TPU v7x, 256 devices: a whole 4x4x8 slice. The times are simulated.
256 devices in a mesh: expert: 32 (over z, y), etp: 8 (over x, core).
Axes of the slice: x: 4, y: 4, z: 8, core: 2. Of those that a mesh axis runs over, the one named last changes fastest.
Arguments:
- tokens: bfloat16 [32768, 2560], P(('expert', 'etp')), may hold values from -6 to 6
- grad_out: bfloat16 [32768, 2560], P(('expert', 'etp')), may hold values from -6 to 6
- router_weight: bfloat16 [2560, 32], replicated, may hold values from -0.125 to 0.125
- expert_choice: int32 [32768, 1], P(('expert', 'etp')), may hold values from 0 to 31; in each aligned block of 128 rows (0 to 127, 128 to 255, ...) at most 6 rows name the same one
- gate_pre: bfloat16 [32, 1536, 4096], P('expert', None, 'etp'), may hold values from -6 to 6
- up_pre: bfloat16 [32, 1536, 4096], P('expert', None, 'etp'), may hold values from -6 to 6
- w_gate: bfloat16 [32, 2560, 4096], P('expert', None, 'etp'), may hold values from -0.125 to 0.125
- w_up: bfloat16 [32, 2560, 4096], P('expert', None, 'etp'), may hold values from -0.125 to 0.125
- w_down: bfloat16 [32, 4096, 2560], P('expert', 'etp'), may hold values from -0.09375 to 0.09375
Outputs:
- token_grad: bfloat16 [32768, 2560], P(('expert', 'etp'))
- router_grad: float32 [2560, 32], replicated
Inputs may be any that keep to these rules, and one draw needn't show every extreme that they name: `expert_choice`: within the 128 tokens of one device no expert is chosen more than 6 times, and in every draw some expert is chosen exactly 6 times by the tokens of some device.
All inputs are finite; a program needn't handle non-finite values.
Results may differ from a plain program's by a relative error of at most 0.015.
Values may be sent and summed in bfloat16 or wider, within the bound.
No kernel may reach another device: no remote copies, remote signals or barrier semaphores. Data moves between devices by JAX's collectives and lax.ppermute only.
A program may use at most 128 MiB of HBM per device.

v0:
```python
import jax
import jax.numpy as jnp
from jax import lax
from jax.sharding import PartitionSpec as P


def local(tokens, grad_out, router_weight, expert_choice, gate_pre, up_pre, w_gate, w_up, w_down):
    width = tokens.shape[1]
    experts = router_weight.shape[1]
    n_expert = lax.axis_size("expert")
    n_etp = lax.axis_size("etp")
    capacity = gate_pre.shape[1] // (n_expert * n_etp)
    hidden = w_down.shape[1]
    contract = (((1,), (1,)), ((), ()))
    chosen_ids = expert_choice[:, 0]
    picked = chosen_ids[:, None] == jnp.arange(experts, dtype=jnp.int32)[None, :]
    logits = jnp.dot(tokens, router_weight, preferred_element_type=jnp.float32)
    score = jax.nn.sigmoid(jnp.sum(jnp.where(picked, logits, 0.0), axis=1))
    counts = picked.astype(jnp.int32)
    earlier = jnp.cumsum(counts, axis=0) - counts
    position = jnp.sum(earlier * counts, axis=1)
    target = chosen_ids * capacity + position
    outgoing = jnp.zeros((experts * capacity, width), jnp.bfloat16).at[target].set(grad_out)
    gate_all = gate_pre[0]
    up_all = up_pre[0]
    gate_w = w_gate[0]
    up_w = w_up[0]
    down_w = w_down[0]
    pooled = lax.all_gather(outgoing, "etp", axis=0, tiled=True)
    pooled = pooled.reshape(n_etp, experts * capacity, width)
    arrived = lax.all_to_all(pooled, "expert", split_axis=1, concat_axis=1, tiled=True)
    d_hidden = lax.dot_general(
        arrived.reshape(n_etp * experts * capacity, width),
        down_w,
        contract,
        preferred_element_type=jnp.float32,
    )
    gate_f = gate_all.astype(jnp.float32)
    up_f = up_all.astype(jnp.float32)
    sig = jax.nn.sigmoid(gate_f)
    d_gate = (d_hidden * up_f * sig * (1.0 + gate_f * (1.0 - sig))).astype(jnp.bfloat16)
    d_up = (d_hidden * gate_f * sig).astype(jnp.bfloat16)
    both = jnp.concatenate([d_gate, d_up], axis=1)
    term = lax.dot_general(both[:, :hidden], gate_w, contract, preferred_element_type=jnp.float32)
    terms = (
        term + lax.dot_general(both[:, hidden:], up_w, contract, preferred_element_type=jnp.float32)
    ).astype(jnp.bfloat16)
    terms = terms.reshape(n_etp, experts * capacity, width)
    swapped = lax.all_to_all(terms, "expert", split_axis=1, concat_axis=1, tiled=True)
    summed = lax.psum_scatter(swapped, "etp", scatter_dimension=0, tiled=True).astype(jnp.float32)
    returned = summed.reshape(experts * capacity, width).astype(jnp.bfloat16)
    fetched = returned[target].astype(jnp.float32)
    inputs = tokens.astype(jnp.float32)
    d_logit = jnp.sum(inputs * fetched, axis=1) * score * (1.0 - score)
    column = lax.dot_general(
        picked.astype(jnp.bfloat16), router_weight, contract, preferred_element_type=jnp.float32
    )
    token_grad = (score[:, None] * fetched + d_logit[:, None] * column).astype(jnp.bfloat16)
    weighted = jnp.where(picked, d_logit[:, None], 0.0)
    local_terms = jnp.dot(
        inputs.T, weighted, precision=lax.Precision.HIGHEST, preferred_element_type=jnp.float32
    )
    router_grad = lax.psum(local_terms, ("expert", "etp"))
    return (token_grad, router_grad)


def solution(mesh):
    placed = (
        P(("expert", "etp"), None),
        P(("expert", "etp"), None),
        P(),
        P(("expert", "etp"), None),
        P("expert", None, "etp"),
        P("expert", None, "etp"),
        P("expert", None, "etp"),
        P("expert", None, "etp"),
        P("expert", "etp", None),
    )
    return jax.shard_map(
        local,
        mesh=mesh,
        in_specs=placed,
        out_specs=(P(("expert", "etp"), None), P()),
        check_vma=False,
    )
```

profile of v0, /device:TPU:1, one launch (start us, length us, event | category | flops | bytes accessed | tf_op | source)
XLA Modules:
  0.0 812.3 jit_solution(2076231841087327123)
XLA Ops:
  7.2 0.0 all-gather.2.cloned.1.call-start
  7.2 0.8 fusion.28
  8.0 0.1 copy.20
  8.1 0.2 reduce_window_sum.11
  8.3 0.1 copy.21
  8.4 0.7 select_reduce_fusion
  9.1 0.7 fusion.33
  9.7 3.2 scatter_custom_fusion
  12.9 0.0 all-gather.2.cloned.1.call-update
  13.0 0.0 reduce-scatter.2.cloned.1.call-start
  13.0 54.4 %all-gather.2.cloned.1.call-done = bf16[1536,2560]{1,0:T(8,128)(2,1)} async-done(((bf16[192,2560]{1,0:T(8,128)(2,1)}), bf16[1536,2560]{1,0:T(8,128)(2,1)}) %all-gather.2.cloned.1.call-update) | async-done | bytes 7864336 | tf_op jit(solution)/shard_map/all_gather | solution.py:29
  67.4 10.7 %copy.22 = bf16[8,192,2560]{2,0,1:T(8,128)(2,1)} copy(bf16[8,192,2560]{2,1,0:T(8,128)(2,1)} %bitcast.44) | data formatting | bytes 15728640 | tf_op jit(solution)/shard_map/reshape | solution.py:30
  78.1 183.8 %all_to_all.10 = bf16[8,192,2560]{2,0,1:T(8,128)(2,1)} all-to-all(bf16[8,192,2560]{2,0,1:T(8,128)(2,1)} %copy.22), channel_id=1, replica_groups=mesh['expert'=32,'etp'=8] {'expert'}, dimensions={1} | all-to-all | bytes 15728640 | tf_op jit(solution)/shard_map/all_to_all | solution.py:31
  261.9 9.0 %copy.23 = bf16[8,192,2560]{2,1,0:T(8,128)(2,1)} copy(bf16[8,192,2560]{2,0,1:T(8,128)(2,1)} %all_to_all.10) | data formatting | bytes 15728640 | tf_op jit(solution)/shard_map/all_to_all | solution.py:31
  270.8 6.7 fusion.14
  277.6 1.7 copy-done.8
  279.3 9.9 %fusion.12 = f32[1536,2560]{1,0:T(8,128)} fusion(bf16[1,2560,512]{2,1,0:T(8,128)(2,1)S(1)} %copy-done, f32[1536,512]{1,0:T(8,128)S(1)} %fusion.14, bf16[1,1536,512]{2,1,0:T(8,128)(2,1)S(1)} %copy-done.6, bf16[1,1536,512]{2,1,0:T(8,128)(2,1)S(1)} %copy-done.7), kind=kOutput, calls=%fused_computation.21 | convolution fusion | flops 4035969024 | bytes 24641536 | tf_op jit(solution)/shard_map/dot_general | solution.py:44
  289.2 15.2 %add_convert_fusion = bf16[1536,2560]{1,0:T(8,128)(2,1)} fusion(f32[1536,2560]{1,0:T(8,128)} %fusion.12, bf16[1,2560,512]{2,1,0:T(8,128)(2,1)} %param.16, f32[1536,512]{1,0:T(8,128)} %copy-done.8, bf16[1,1536,512]{2,1,0:T(8,128)(2,1)} %param.13), kind=kOutput, calls=%fused_computation.2 | convolution fusion | flops 4039901184 | bytes 30932992 | tf_op jit(solution)/shard_map/dot_general | solution.py:46
  304.5 10.6 %copy.24 = bf16[8,192,2560]{2,0,1:T(8,128)(2,1)} copy(bf16[8,192,2560]{2,1,0:T(8,128)(2,1)} %bitcast.45) | data formatting | bytes 15728640 | tf_op jit(solution)/shard_map/reshape | solution.py:48
  315.1 177.6 %all_to_all.11 = bf16[8,192,2560]{2,0,1:T(8,128)(2,1)} all-to-all(bf16[8,192,2560]{2,0,1:T(8,128)(2,1)} %copy.24), channel_id=1, replica_groups=mesh['expert'=32,'etp'=8] {'expert'}, dimensions={1} | all-to-all | bytes 15728640 | tf_op jit(solution)/shard_map/all_to_all | solution.py:49
  492.6 8.7 %copy.25 = bf16[8,192,2560]{2,1,0:T(8,128)(2,1)} copy(bf16[8,192,2560]{2,0,1:T(8,128)(2,1)} %all_to_all.11) | data formatting | bytes 15728640 | tf_op jit(solution)/shard_map/all_to_all | solution.py:49
  501.4 0.0 all-reduce.2.cloned.1.call-start
  501.5 1.0 copy-done.2
  502.5 0.0 copy-done.3
  502.5 0.3 fusion.24
  502.8 48.4 %reduce-scatter.2.cloned.1.call-done = bf16[1,192,2560]{2,1,0:T(8,128)(2,1)} async-done(((bf16[8,192,2560]{2,1,0:T(8,128)(2,1)}), bf16[1,192,2560]{2,1,0:T(8,128)(2,1)}) %reduce-scatter.2.cloned.1.call-update) | async-done | bytes 983056 | tf_op jit(solution)/shard_map/reduce_scatter | solution.py:50
  551.2 3.9 gather_fusion
  555.2 1.3 fusion.23
  556.5 1.1 convolution_bitcast_fusion
  557.7 2.3 fusion.1
  560.0 244.0 %all-reduce.2.cloned.1.call-done = f32[2560,32]{0,1:T(8,128)} async-done(((f32[2560,32]{0,1:T(8,128)}), f32[2560,32]{0,1:T(8,128)}) %all-reduce.2.cloned.1.call-update) | async-done | bytes 327696 | tf_op jit(solution)/shard_map/psum | solution.py:63
  804.0 1.7 copy.27
  (19 shorter events, 0.1 us)
Async XLA Ops:
  7.2 272.1 %copy-start = (bf16[1,2560,512]{2,1,0:T(8,128)(2,1)S(1)}, bf16[1,2560,512]{2,1,0:T(8,128)(2,1)}, u32[]{:S(2)}) copy-start(bf16[1,2560,512]{2,1,0:T(8,128)(2,1)} %param.15) | copy-start | bytes 7864324
  7.2 60.2 %all-gather.2.cloned.1.call-start = ((), (), s32[]{:S(2)}) async-start(), calls=%async_computation.3 | async-start | bytes 8847360 | tf_op jit(solution)/shard_map/all_gather | solution.py:29
  13.0 538.3 %reduce-scatter.2.cloned.1.call-start = ((), (), s32[]{:S(2)}) async-start(), calls=%async_computation.4 | async-start | bytes 8847360 | tf_op jit(solution)/shard_map/reduce_scatter | solution.py:50
  261.9 9.0 %copy-start.5 = (bf16[1,512,2560]{2,1,0:T(8,128)(2,1)S(1)}, bf16[1,512,2560]{2,1,0:T(8,128)(2,1)}, u32[]{:S(2)}) copy-start(bf16[1,512,2560]{2,1,0:T(8,128)(2,1)} %param.17) | copy-start | bytes 7864324
  270.8 8.5 %copy-start.6 = (bf16[1,1536,512]{2,1,0:T(8,128)(2,1)S(1)}, bf16[1,1536,512]{2,1,0:T(8,128)(2,1)}, u32[]{:S(2)}) copy-start(bf16[1,1536,512]{2,1,0:T(8,128)(2,1)} %param.14) | copy-start | bytes 4718596
  270.8 8.5 %copy-start.7 = (bf16[1,1536,512]{2,1,0:T(8,128)(2,1)S(1)}, bf16[1,1536,512]{2,1,0:T(8,128)(2,1)}, u32[]{:S(2)}) copy-start(bf16[1,1536,512]{2,1,0:T(8,128)(2,1)} %param.13) | copy-start | bytes 4718596
  277.6 1.7 copy-start.8
  501.4 1.1 copy-start.2
  501.4 1.1 copy-start.3
  501.4 1.1 copy-start.4
  501.4 302.6 %all-reduce.2.cloned.1.call-start = ((), (), s32[]{:S(2)}) async-start(), calls=%async_computation.5 | async-start | bytes 655360 | tf_op jit(solution)/shard_map/psum | solution.py:63
  551.2 254.5 %copy-start.1 = (bf16[1,2560,512]{2,1,0:T(8,128)(2,1)S(1)}, bf16[1,2560,512]{2,1,0:T(8,128)(2,1)}, u32[]{:S(2)}) copy-start(bf16[1,2560,512]{2,1,0:T(8,128)(2,1)} %param.15) | copy-start | bytes 7864324
Sparse Core Ops, SparseCore 0:
  13.1 54.2 all-gather.1
  501.5 49.6 reduce-scatter.1
  557.8 246.1 all-reduce.1
where the time goes:
time: 813 us; the launch traced here: 812 us
  blocking collectives  361 us (44%)
  waiting for transfers between devices  347 us (43%)
  local copies, waits for them, and re-layouts  50.8 us (6%)
  matrix products  35.6 us (4%)
  between operations  13.8 us (2%)
    psum x1, waiting for transfers between devices, local(): router_grad = lax.psum(local_terms, ('expert', 'etp'))  244 us
    all_to_all x1, blocking collectives, local(): lax.all_to_all(pooled, 'expert', split_axis=1, concat_axis=1, tiled=True)  184 us
    all_to_all x1, blocking collectives, local(): lax.all_to_all(terms, 'expert', split_axis=1, concat_axis=1, tiled=True)  178 us
    all_gather x1, waiting for transfers between devices, local(): pooled = lax.all_gather(outgoing, 'etp', axis=0, tiled=True)  54.4 us
    reduce_scatter x1, waiting for transfers between devices, local(): lax.psum_scatter(swapped, 'etp', scatter_dimension=0, tiled=True)  48.4 us
  transfers between devices with their start and end apart: 3, of which 3 were waited for; matrix products, arithmetic and copies ran while one was open for 0% of the time, Pallas kernels for 0%

commit v1 on v0

--- a/solution.py
+++ b/solution.py
@@ -26,7 +26,27 @@
     gate_w = w_gate[0]
     up_w = w_up[0]
     down_w = w_down[0]
-    pooled = lax.all_gather(outgoing, "etp", axis=0, tiled=True)
+    plain = lax.axis_index("etp")
+    taken_in = lax.axis_size("etp")
+    carry, block_next, known = (taken_in, plain, outgoing.shape[0])
+    all_blocks = [(t, (t + 1) % carry) for t in range(carry)]
+    pooled = jnp.zeros(
+        (*outgoing.shape[:0], carry * known, *outgoing.shape[0 + 1 :]), outgoing.dtype
+    )
+    pooled = lax.dynamic_update_slice_in_dim(pooled, outgoing, block_next * known, axis=0)
+    xs_all = [(t, (t - 1) % carry) for t in range(carry)]
+    p_next = new = outgoing
+    row_out = carry // 2
+    for j in range(1, row_out + 1):
+        p_next = lax.ppermute(p_next, "etp", all_blocks)
+        pooled = lax.dynamic_update_slice_in_dim(
+            pooled, p_next, (block_next - j) % carry * known, axis=0
+        )
+        if j < carry - row_out:
+            new = lax.ppermute(new, "etp", xs_all)
+            pooled = lax.dynamic_update_slice_in_dim(
+                pooled, new, (block_next + j) % carry * known, axis=0
+            )
     pooled = pooled.reshape(n_etp, experts * capacity, width)
     arrived = lax.all_to_all(pooled, "expert", split_axis=1, concat_axis=1, tiled=True)
     d_hidden = lax.dot_general(

time: 813 us -> 820 us (level)
  local copies, waits for them, and re-layouts: 50.8 us -> 66.1 us
  starting transfers between devices: 0.12 us -> 15.3 us
  waiting for transfers between devices: 347 us -> 332 us
  blocking collectives: 361 us -> 352 us
    all_gather x1 -> x0, waiting for transfers between devices: 54.4 us -> none  [local(): pooled = lax.all_gather(outgoing, 'etp', axis=0, tiled=True)]
    ppermute x0 -> x7, waiting for transfers between devices: none -> 25.4 us  [the longest x4 23 us: local(): p_next = lax.ppermute(p_next, 'etp', all_blocks)]
    ppermute x0 -> x7, starting transfers between devices: none -> 15.2 us  [the longest x4 9.94 us: local(): p_next = lax.ppermute(p_next, 'etp', all_blocks)]
    reduce_scatter x1, waiting for transfers between devices: 48.4 us -> 62.9 us  [local(): lax.psum_scatter(swapped, 'etp', scatter_dimension=0, tiled=True)]
    dynamic_update_slice x0 -> x8, local copies, waits for them, and re-layouts: none -> 11.8 us  [the longest x4 6.52 us: local(): lax.dynamic_update_slice_in_dim(pooled, p_next, (block_next - j) % carry...]
  transfers between devices with their start and end apart: 3 -> 9, of which waited for: 3 -> 8; matrix products, arithmetic and copies ran while one was open for 0% -> 2% of each run, Pallas kernels for 0% -> 0%
where the time goes in v1:
time: 820 us; the launch traced here: 819 us
  blocking collectives  352 us (43%)
  waiting for transfers between devices  332 us (40%)
  local copies, waits for them, and re-layouts  66.1 us (8%)
  matrix products  35.7 us (4%)
  starting transfers between devices  15.3 us (2%)
  between operations  14.1 us (2%)
    psum x1, waiting for transfers between devices, local(): router_grad = lax.psum(local_terms, ('expert', 'etp'))  244 us
    all_to_all x1, blocking collectives, local(): lax.all_to_all(pooled, 'expert', split_axis=1, concat_axis=1, tiled=True)  179 us
    all_to_all x1, blocking collectives, local(): lax.all_to_all(terms, 'expert', split_axis=1, concat_axis=1, tiled=True)  173 us
    reduce_scatter x1, waiting for transfers between devices, local(): lax.psum_scatter(swapped, 'etp', scatter_dimension=0, tiled=True)  62.9 us
    ppermute x4, waiting for transfers between devices, local(): p_next = lax.ppermute(p_next, 'etp', all_blocks)  23 us
  transfers between devices with their start and end apart: 9, of which 8 were waited for; matrix products, arithmetic and copies ran while one was open for 2% of the time, Pallas kernels for 0%

profile of v1, /device:TPU:1, one launch (start us, length us, event | category | flops | bytes accessed | tf_op | source)
XLA Modules:
  0.0 819.4 jit_solution(1929266241360226068)
XLA Ops:
  9.7 3.1 scatter_custom_fusion
  12.8 2.6 collective-permute-start
  16.1 10.7 %collective-permute-done = bf16[192,2560]{1,0:T(8,128)(2,1)} collective-permute-done((bf16[192,2560]{1,0:T(8,128)(2,1)}, bf16[192,2560]{1,0:T(8,128)(2,1)}, u32[]{:S(2)}, u32[]{:S(2)}) %collective-permute-start) | collective-permute-done | bytes 983072 | tf_op jit(solution)/shard_map/ppermute | solution.py:41
  26.8 2.5 collective-permute-start.2
  29.6 1.6 collective-permute-start.3
  31.2 3.6 broadcast_in_dim.27
  35.8 4.8 collective-permute-done.2
  40.6 2.5 collective-permute-start.4
  43.1 2.2 constant_dynamic-update-slice_fusion.5
  45.4 2.2 constant_dynamic-update-slice_fusion.4
  47.6 3.1 collective-permute-start.5
  50.7 2.2 constant_dynamic-update-slice_fusion.3
  52.9 1.6 collective-permute-done.4
  54.5 2.4 collective-permute-start.6
  58.9 2.2 collective-permute-done.5
  62.1 5.8 collective-permute-done.6
  68.9 10.7 %copy.21 = bf16[8,192,2560]{2,0,1:T(8,128)(2,1)} copy(bf16[8,192,2560]{2,1,0:T(8,128)(2,1)} %bitcast.3) | data formatting | bytes 15728640 | tf_op jit(solution)/shard_map/reshape | solution.py:50
  79.6 178.7 %all_to_all.10 = bf16[8,192,2560]{2,0,1:T(8,128)(2,1)} all-to-all(bf16[8,192,2560]{2,0,1:T(8,128)(2,1)} %copy.21), channel_id=1, replica_groups=mesh['expert'=32,'etp'=8] {'expert'}, dimensions={1} | all-to-all | bytes 15728640 | tf_op jit(solution)/shard_map/all_to_all | solution.py:51
  258.3 9.0 %copy.22 = bf16[8,192,2560]{2,1,0:T(8,128)(2,1)} copy(bf16[8,192,2560]{2,0,1:T(8,128)(2,1)} %all_to_all.10) | data formatting | bytes 15728640 | tf_op jit(solution)/shard_map/all_to_all | solution.py:51
  267.3 6.7 fusion.14
  274.1 1.7 copy-done.9
  275.8 9.9 %fusion.12 = f32[1536,2560]{1,0:T(8,128)} fusion(bf16[1,2560,512]{2,1,0:T(8,128)(2,1)S(1)} %copy-done, f32[1536,512]{1,0:T(8,128)S(1)} %fusion.14, bf16[1,1536,512]{2,1,0:T(8,128)(2,1)S(1)} %copy-done.7, bf16[1,1536,512]{2,1,0:T(8,128)(2,1)S(1)} %copy-done.8), kind=kOutput, calls=%fused_computation.21 | convolution fusion | flops 4035969024 | bytes 24641536 | tf_op jit(solution)/shard_map/dot_general | solution.py:64
  285.7 15.3 %add_convert_fusion = bf16[1536,2560]{1,0:T(8,128)(2,1)} fusion(f32[1536,2560]{1,0:T(8,128)} %fusion.12, bf16[1,2560,512]{2,1,0:T(8,128)(2,1)} %param.16, f32[1536,512]{1,0:T(8,128)} %copy-done.9, bf16[1,1536,512]{2,1,0:T(8,128)(2,1)} %param.13), kind=kOutput, calls=%fused_computation.2 | convolution fusion | flops 4039901184 | bytes 30932992 | tf_op jit(solution)/shard_map/dot_general | solution.py:66
  301.0 10.6 %copy.23 = bf16[8,192,2560]{2,0,1:T(8,128)(2,1)} copy(bf16[8,192,2560]{2,1,0:T(8,128)(2,1)} %bitcast.44) | data formatting | bytes 15728640 | tf_op jit(solution)/shard_map/reshape | solution.py:68
  311.6 173.5 %all_to_all.11 = bf16[8,192,2560]{2,0,1:T(8,128)(2,1)} all-to-all(bf16[8,192,2560]{2,0,1:T(8,128)(2,1)} %copy.23), channel_id=1, replica_groups=mesh['expert'=32,'etp'=8] {'expert'}, dimensions={1} | all-to-all | bytes 15728640 | tf_op jit(solution)/shard_map/all_to_all | solution.py:69
  485.0 8.7 %copy.24 = bf16[8,192,2560]{2,1,0:T(8,128)(2,1)} copy(bf16[8,192,2560]{2,0,1:T(8,128)(2,1)} %all_to_all.11) | data formatting | bytes 15728640 | tf_op jit(solution)/shard_map/all_to_all | solution.py:69
  495.2 62.9 %reduce-scatter.2.cloned.1.call-done = bf16[1,192,2560]{2,1,0:T(8,128)(2,1)} async-done(((bf16[8,192,2560]{2,1,0:T(8,128)(2,1)}), bf16[1,192,2560]{2,1,0:T(8,128)(2,1)}) %reduce-scatter.2.cloned.1.call-update) | async-done | bytes 983056 | tf_op jit(solution)/shard_map/reduce_scatter | solution.py:70
  558.1 3.9 gather_fusion
  562.0 1.3 fusion.23
  564.5 2.3 fusion.1
  566.8 244.0 %all-reduce.2.cloned.1.call-done = f32[2560,32]{0,1:T(8,128)} async-done(((f32[2560,32]{0,1:T(8,128)}), f32[2560,32]{0,1:T(8,128)}) %all-reduce.2.cloned.1.call-update) | async-done | bytes 327696 | tf_op jit(solution)/shard_map/psum | solution.py:83
  810.8 1.7 copy.34
  (41 shorter events, 11.2 us)
Async XLA Ops:
  7.2 268.6 %copy-start = (bf16[1,2560,512]{2,1,0:T(8,128)(2,1)S(1)}, bf16[1,2560,512]{2,1,0:T(8,128)(2,1)}, u32[]{:S(2)}) copy-start(bf16[1,2560,512]{2,1,0:T(8,128)(2,1)} %param.15) | copy-start | bytes 7864324
  7.2 550.9 %reduce-scatter.2.cloned.1.call-start = ((), (), s32[]{:S(2)}) async-start(), calls=%async_computation.3 | async-start | bytes 8847360 | tf_op jit(solution)/shard_map/reduce_scatter | solution.py:70
  12.8 14.0 %collective-permute-start = (bf16[192,2560]{1,0:T(8,128)(2,1)}, bf16[192,2560]{1,0:T(8,128)(2,1)}, u32[]{:S(2)}, u32[]{:S(2)}) collective-permute-start(bf16[192,2560]{1,0:T(8,128)(2,1)} %scatter_custom_fusion), channel_id=1, source_target_pairs={{0,1},{1,2},{2,3},{3,4},{4,5},{5,6},{6,7},{7,0},{8,9},{9,10},{10,1... | collective-permute-start | bytes 2949128 | tf_op jit(solution)/shard_map/ppermute | solution.py:41
  15.4 14.1 %collective-permute-start.1 = (bf16[192,2560]{1,0:T(8,128)(2,1)}, bf16[192,2560]{1,0:T(8,128)(2,1)}, u32[]{:S(2)}, u32[]{:S(2)}) collective-permute-start(bf16[192,2560]{1,0:T(8,128)(2,1)} %scatter_custom_fusion), channel_id=1, source_target_pairs={{0,7},{1,0},{2,1},{3,2},{4,3},{5,4},{6,5},{7,6},{8,15},{9,8},{10,9... | collective-permute-start | bytes 2949128 | tf_op jit(solution)/shard_map/ppermute | solution.py:46
  26.8 13.8 %collective-permute-start.2 = (bf16[192,2560]{1,0:T(8,128)(2,1)}, bf16[192,2560]{1,0:T(8,128)(2,1)}, u32[]{:S(2)}, u32[]{:S(2)}) collective-permute-start(bf16[192,2560]{1,0:T(8,128)(2,1)} %collective-permute-done), channel_id=1, source_target_pairs={{0,1},{1,2},{2,3},{3,4},{4,5},{5,6},{6,7},{7,0},{8,9},{9,10},{10,1... | collective-permute-start | bytes 2949128 | tf_op jit(solution)/shard_map/ppermute | solution.py:41
  29.3 5.5 copy-start.3
  29.6 18.0 %collective-permute-start.3 = (bf16[192,2560]{1,0:T(8,128)(2,1)}, bf16[192,2560]{1,0:T(8,128)(2,1)S(1)}, u32[]{:S(2)}, u32[]{:S(2)}) collective-permute-start(bf16[192,2560]{1,0:T(8,128)(2,1)} %collective-permute-done.1), channel_id=1, source_target_pairs={{0,7},{1,0},{2,1},{3,2},{4,3},{5,4},{6,5},{7,6},{8,15},{9,8},{10,9... | collective-permute-start | bytes 2949128 | tf_op jit(solution)/shard_map/ppermute | solution.py:46
  40.6 13.8 %collective-permute-start.4 = (bf16[192,2560]{1,0:T(8,128)(2,1)}, bf16[192,2560]{1,0:T(8,128)(2,1)S(1)}, u32[]{:S(2)}, u32[]{:S(2)}) collective-permute-start(bf16[192,2560]{1,0:T(8,128)(2,1)} %collective-permute-done.2), channel_id=1, source_target_pairs={{0,1},{1,2},{2,3},{3,4},{4,5},{5,6},{6,7},{7,0},{8,9},{9,10},{10,1... | collective-permute-start | bytes 2949128 | tf_op jit(solution)/shard_map/ppermute | solution.py:41
  47.6 13.5 %collective-permute-start.5 = (bf16[192,2560]{1,0:T(8,128)(2,1)S(1)}, bf16[192,2560]{1,0:T(8,128)(2,1)S(1)}, u32[]{:S(2)}, u32[]{:S(2)}) collective-permute-start(bf16[192,2560]{1,0:T(8,128)(2,1)S(1)} %collective-permute-done.3), channel_id=1, source_target_pairs={{0,7},{1,0},{2,1},{3,2},{4,3},{5,4},{6,5},{7,6},{8,15},{9,8},{10,9... | collective-permute-start | bytes 2949128 | tf_op jit(solution)/shard_map/ppermute | solution.py:46
  54.5 13.4 %collective-permute-start.6 = (bf16[192,2560]{1,0:T(8,128)(2,1)S(1)}, bf16[192,2560]{1,0:T(8,128)(2,1)S(1)}, u32[]{:S(2)}, u32[]{:S(2)}) collective-permute-start(bf16[192,2560]{1,0:T(8,128)(2,1)S(1)} %collective-permute-done.4), channel_id=1, source_target_pairs={{0,1},{1,2},{2,3},{3,4},{4,5},{5,6},{6,7},{7,0},{8,9},{9,10},{10,1... | collective-permute-start | bytes 2949128 | tf_op jit(solution)/shard_map/ppermute | solution.py:41
  258.3 9.0 %copy-start.6 = (bf16[1,512,2560]{2,1,0:T(8,128)(2,1)S(1)}, bf16[1,512,2560]{2,1,0:T(8,128)(2,1)}, u32[]{:S(2)}) copy-start(bf16[1,512,2560]{2,1,0:T(8,128)(2,1)} %param.17) | copy-start | bytes 7864324
  267.3 8.5 %copy-start.7 = (bf16[1,1536,512]{2,1,0:T(8,128)(2,1)S(1)}, bf16[1,1536,512]{2,1,0:T(8,128)(2,1)}, u32[]{:S(2)}) copy-start(bf16[1,1536,512]{2,1,0:T(8,128)(2,1)} %param.14) | copy-start | bytes 4718596
  267.3 8.5 %copy-start.8 = (bf16[1,1536,512]{2,1,0:T(8,128)(2,1)S(1)}, bf16[1,1536,512]{2,1,0:T(8,128)(2,1)}, u32[]{:S(2)}) copy-start(bf16[1,1536,512]{2,1,0:T(8,128)(2,1)} %param.13) | copy-start | bytes 4718596
  274.0 1.7 copy-start.9
  493.8 1.1 copy-start.2
  493.8 1.1 copy-start.4
  493.8 1.1 copy-start.5
  493.8 317.0 %all-reduce.2.cloned.1.call-start = ((), (), s32[]{:S(2)}) async-start(), calls=%async_computation.4 | async-start | bytes 655360 | tf_op jit(solution)/shard_map/psum | solution.py:83
  558.1 254.5 %copy-start.1 = (bf16[1,2560,512]{2,1,0:T(8,128)(2,1)S(1)}, bf16[1,2560,512]{2,1,0:T(8,128)(2,1)}, u32[]{:S(2)}) copy-start(bf16[1,2560,512]{2,1,0:T(8,128)(2,1)} %param.15) | copy-start | bytes 7864324
Sparse Core Ops, SparseCore 0:
  493.9 64.1 reduce-scatter.1
  564.7 246.1 all-reduce.1
